TPU v7x, 32 devices: a whole 2x2x4 slice. The times are simulated.
32 devices in a mesh: row: 8 (over z, core), col: 4 (over y, x).
Axes of the slice: x: 2, y: 2, z: 4, core: 2. Of those that a mesh axis runs over, the one named last changes fastest.
Arguments:
- trials: float32 [2, 512, 1024], P(None, 'col', 'row'), may hold values from -6 to 6
- valence_orb: float32 [512, 8192], P('col', 'row'), may hold values from -0.25 to 0.25
- conduction_orb: float32 [1024, 8192], P('row', 'col'), may hold values from -0.1875 to 0.1875
- screened: float32 [8192, 8192], P('row', 'col'), may hold values from -0.5 to 0.5
Outputs:
- applied: float32 [2, 512, 1024], P(None, 'col', 'row')
All inputs are finite; a program needn't handle non-finite values.
Results may differ from a plain program's by a relative error of at most 0.0003.
Values sent between devices are 32-bit elements; how exact they have to be, the bound alone decides.
A program may use at most 64 MiB of HBM per device.

v0:
```python
import functools

import jax
import jax.numpy as jnp
from jax import lax
from jax.experimental import pallas as pl
from jax.experimental.pallas import tpu as pltpu
from jax.sharding import PartitionSpec as P

F32 = jnp.float32
BF16 = jnp.bfloat16


def split(x):
    hi = x.astype(BF16)
    return hi, (x - hi.astype(F32)).astype(BF16)


def dot3(a_hi, a_lo, b_hi, b_lo, dims=((1,), (0,))):
    def one(a, b):
        return lax.dot_general(a, b, (dims, ((), ())), preferred_element_type=F32)

    return one(a_hi, b_hi) + (one(a_lo, b_hi) + one(a_hi, b_lo))


def kernel(
    R, Q, K,
    t_ref, v_ref, co_ref, s_hbm, out_ref,
    t_buf, t_hi, t_lo, v_all, v_hi, v_lo, vt_hi, vt_lo, co_buf, co_hi, co_lo, s_buf,
    u_hi, u_lo, psend, precv, osum, xrecv, zbuf, zrecv,
    t_recv, t_zs, t_xs, t_ps, v_recv, v_send, co_recv, co_own, co_rel, co_fwd,
    s_sem, p_send, p_recv, x_send, x_recv, z_send, z_recv,
):
    NT, vb, cb = t_ref.shape
    V = vb * Q
    L = R // 2
    nw = co_buf.shape[3]
    row, q = lax.axis_index("row"), lax.axis_index("col")
    p, c = row // 2, row % 2
    mypos = c * L + p
    partner = (p * 2 + (1 - c), q)

    def line(pp):
        return (pp * 2 + c, q)

    def peer(qq):
        return (row, qq)

    def remote(src, dst, ss, rs, dev):
        return pltpu.make_async_remote_copy(
            src_ref=src, dst_ref=dst, send_sem=ss, recv_sem=rs,
            device_id=dev, device_id_type=pl.DeviceIdType.MESH,
        )

    barrier = pltpu.get_barrier_semaphore()
    others = [partner]
    others += [line((p + d) % L) for d in range(1, L)]
    others += [peer((q + d) % Q) for d in range(1, Q)]
    for dev in others:
        pl.semaphore_signal(barrier, inc=1, device_id=dev, device_id_type=pl.DeviceIdType.MESH)
    pl.semaphore_wait(barrier, len(others))

    def t_line(d):
        return remote(t_ref, t_buf.at[mypos, q], t_zs.at[d], t_recv.at[mypos, q], line((p + d) % L))

    def t_peer(j, d):
        pos = c * L + (p + L - j) % L
        src = t_ref if j == 0 else t_buf.at[pos, q]
        return remote(src, t_buf.at[pos, q], t_xs.at[j, d], t_recv.at[pos, q], peer((q + d) % Q))

    def t_partner(j, d):
        pos = c * L + (p + L - j) % L
        qq = (q + Q - d) % Q
        src = t_ref if (j == 0 and d == 0) else t_buf.at[pos, qq]
        return remote(src, t_buf.at[pos, qq], t_ps.at[j, d], t_recv.at[pos, qq], partner)

    def t_wait(pos, qq):
        remote(t_buf.at[pos, qq], t_buf.at[pos, qq], t_zs.at[0], t_recv.at[pos, qq], partner).wait_recv()

    def v_peer(d):
        return remote(v_ref, v_all.at[q], v_send.at[d], v_recv.at[q], peer((q + d) % Q))

    def own_to(k, d):
        lanes = pl.ds(pl.multiple_of(k * nw, nw), nw)
        sign = 1 if d > 0 else -1
        return remote(
            co_ref.at[:, lanes], co_buf.at[k, mypos],
            co_own.at[k, abs(d) - 1 + (2 if sign < 0 else 0)], co_recv.at[k, mypos],
            line(jnp.clip(p + d, 0, L - 1)),
        )

    def own_partner(k):
        lanes = pl.ds(pl.multiple_of(k * nw, nw), nw)
        return remote(
            co_ref.at[:, lanes], co_buf.at[k, mypos], co_own.at[k, 4], co_recv.at[k, mypos], partner
        )

    def own_cases():
        for d in (1, 2):
            if d < L:
                yield d, p + d <= L - 1
                yield -d, p - d >= 0

    def send_own(k):
        for d, ok in own_cases():
            @pl.when(ok)
            def _():
                own_to(k, d).start()
        own_partner(k).start()

    def relay_right(pp):
        return jnp.logical_and(p - pp >= 2, p < L - 1)

    def relay_left(pp):
        return jnp.logical_and(pp - p >= 2, p > 0)

    def relay_copy(k, pp, to):
        pos = c * L + pp
        return remote(
            co_buf.at[k, pos], co_buf.at[k, pos], co_rel.at[k, pp], co_recv.at[k, pos],
            line(jnp.clip(to, 0, L - 1)),
        )

    def co_wait(k, pos):
        remote(co_buf.at[k, pos], co_buf.at[k, pos], co_own.at[k, 4], co_recv.at[k, pos], partner).wait_recv()

    def relay(k):
        for pp in range(L):
            for ok, to in ((relay_right(pp), p + 1), (relay_left(pp), p - 1)):
                @pl.when(ok)
                def _():
                    co_wait(k, c * L + pp)
                    relay_copy(k, pp, to).start()

    def fwd_copy(k, pp):
        pos = c * L + pp
        return remote(co_buf.at[k, pos], co_buf.at[k, pos], co_fwd.at[k, pp], co_recv.at[k, pos], partner)

    def forward(k):
        for pp in range(L):
            @pl.when(pp != p)
            def _():
                @pl.when(jnp.logical_not(jnp.logical_or(relay_right(pp), relay_left(pp))))
                def _():
                    co_wait(k, c * L + pp)
                fwd_copy(k, pp).start()

    def s_copy(k, slot):
        lanes = pl.ds(pl.multiple_of(k * nw, nw), nw)
        return pltpu.make_async_copy(s_hbm.at[:, lanes], s_buf.at[slot], s_sem.at[slot])

    for d in range(1, L):
        t_line(d).start()
    for d in range(1, Q):
        t_peer(0, d).start()
    t_partner(0, 0).start()
    ahead = [0]

    def more_own(k):
        while ahead[0] < min(k, K):
            send_own(ahead[0])
            ahead[0] += 1

    def more(fn, k):
        if k < K:
            fn(k)

    more_own(3)
    s_copy(0, 0).start()
    t_buf[mypos, q] = t_ref[...]
    v_all[q] = v_ref[...]
    for k in range(K):
        co_buf[k, mypos] = co_ref[:, k * nw : (k + 1) * nw]
    for j in range(1, L):
        t_wait(c * L + (p + L - j) % L, q)
        for d in range(1, Q):
            t_peer(j, d).start()
        t_partner(j, 0).start()
    for d in range(1, Q):
        v_peer(d).start()
    more(relay, 0)
    more_own(4)
    for j in range(L):
        for d in range(1, Q):
            t_wait(c * L + (p + L - j) % L, (q + Q - d) % Q)
            t_partner(j, d).start()
    more(relay, 1)
    more(forward, 0)
    more_own(5)
    for pp in range(L):
        for qq in range(Q):
            t_wait((1 - c) * L + pp, qq)
    for pos in range(R):
        for qq in range(Q):
            for t in range(NT):
                hi, lo = split(t_buf[pos, qq, t])
                rows, lanes = slice(t * V + qq * vb, t * V + (qq + 1) * vb), slice(pos * cb, (pos + 1) * cb)
                t_hi[rows, lanes] = hi
                t_lo[rows, lanes] = lo

    def lanes_of(k):
        return pl.ds(pl.multiple_of(k * nw, nw), nw)

    def encode_half(k):
        for pp in range(L):
            co_wait(k, (1 - c) * L + pp)
        lanes = lanes_of(k)
        for pos in range(R):
            hi, lo = split(co_buf[k, pos])
            co_hi[pos * cb : (pos + 1) * cb, lanes] = hi
            co_lo[pos * cb : (pos + 1) * cb, lanes] = lo
        half = dot3(t_hi[...], t_lo[...], co_hi[:, lanes], co_lo[:, lanes])
        hi, lo = split(half)
        u_hi[:, lanes] = hi
        u_lo[:, lanes] = lo

    def project(slot, k, t):
        lanes = lanes_of(k)
        rows = pl.ds(pl.multiple_of(t * V, V), V)
        pairs = s_buf[slot] * dot3(vt_hi[...], vt_lo[...], u_hi[rows, lanes], u_lo[rows, lanes])
        p_hi, p_lo = split(pairs)
        hi, lo = split(dot3(v_hi[...], v_lo[...], p_hi, p_lo))
        u_hi[rows, lanes] = hi
        u_lo[rows, lanes] = lo

    more(relay, 2)
    more(forward, 1)
    more_own(6)
    encode_half(0)
    more(relay, 3)
    more(forward, 2)
    more_own(7)
    more(encode_half, 1)
    for d in range(1, Q):
        qq = (q + Q - d) % Q
        remote(v_all.at[qq], v_all.at[qq], v_send.at[0], v_recv.at[qq], partner).wait_recv()
    for qq in range(Q):
        hi, lo = split(v_all[qq])
        v_hi[qq * vb : (qq + 1) * vb, :] = hi
        v_lo[qq * vb : (qq + 1) * vb, :] = lo
    hi, lo = split(v_all[...].reshape(V, v_all.shape[2]).T)
    vt_hi[...] = hi
    vt_lo[...] = lo

    both = K // 2
    steps = both + NT * (K - both)

    def next_screened(i):
        @pl.when(i + 1 < steps)
        def _():
            later = jnp.where(i + 1 < both, i + 1, both + (i + 1 - both) % (K - both))
            s_copy(later, (i + 1) % 2).start()

    def stage(s, carry):
        @pl.when(s + 7 < K)
        def _():
            send_own(s + 7)

        @pl.when(s + 4 < K)
        def _():
            relay(s + 4)

        @pl.when(s + 3 < K)
        def _():
            forward(s + 3)

        @pl.when(s + 2 < K)
        def _():
            encode_half(s + 2)

        s_copy(s, s % 2).wait()
        next_screened(s)

        def one(t, carry):
            project(s % 2, s, t)
            return carry

        return lax.fori_loop(0, jnp.where(s < both, NT, 1), one, carry)

    lax.fori_loop(0, K, stage, 0)

    half_c = L * cb

    def decode(t, par):
        rows = slice(t * V, (t + 1) * V)
        cols = pl.ds(pl.multiple_of(par * half_c, half_c), half_c)
        return dot3(u_hi[rows, :], u_lo[rows, :], co_hi[cols, :], co_lo[cols, :], ((1,), (1,)))

    def p_copy(t):
        return remote(psend.at[t], precv.at[t], p_send.at[t], p_recv.at[t], partner)

    def x_copy(t, d):
        to = (q + d) % Q
        return remote(osum.at[t, to], xrecv.at[t, d], x_send.at[t, d], x_recv.at[t, d], peer(to))

    def z_copy(t, d):
        to = (p + d) % L
        return remote(zbuf.at[t, to], zrecv.at[t, d], z_send.at[t, d], z_recv.at[t, d], line(to))

    def to_partner(t):
        psend[t] = decode(t, 1 - c)
        p_copy(t).start()

    def to_peers(t):
        own = decode(t, c)
        p_copy(t).wait_recv()
        for qq in range(Q):
            osum[t, qq] = own[qq * vb : (qq + 1) * vb, :] + precv[t, qq * vb : (qq + 1) * vb, :]
        for d in range(Q - 1, 0, -1):
            x_copy(t, d).start()

    def to_line(t):
        total = osum[t, q]
        for d in range(Q - 1, 0, -1):
            x_copy(t, d).wait_recv()
            total = total + xrecv[t, d]
        for pp in range(L):
            zbuf[t, pp] = total[:, pp * cb : (pp + 1) * cb]
        for d in range(1, L):
            z_copy(t, d).start()

    def finish(t):
        final = zbuf[t, p]
        for d in range(1, L):
            z_copy(t, d).wait_recv()
            final = final + zrecv[t, d]
        out_ref[t] = final

    for t in range(NT):
        if t > 0:
            def later_stage(s, carry):
                i = both + t * (K - both) + s
                s_copy(both + s, i % 2).wait()
                next_screened(i)
                project(i % 2, both + s, t)
                return carry

            lax.fori_loop(0, K - both, later_stage, 0)
        to_partner(t)
        if t > 0:
            to_line(t - 1)
        to_peers(t)
    to_line(NT - 1)
    for t in range(NT):
        finish(t)

    for d in range(1, L):
        t_line(d).wait_send()
        for t in range(NT):
            z_copy(t, d).wait_send()
    for d in range(1, Q):
        v_peer(d).wait_send()
        for t in range(NT):
            x_copy(t, d).wait_send()
    for t in range(NT):
        p_copy(t).wait_send()
    for j in range(L):
        for d in range(1, Q):
            t_peer(j, d).wait_send()
        for d in range(Q):
            t_partner(j, d).wait_send()

    def drain(k, carry):
        for d, ok in own_cases():
            @pl.when(ok)
            def _():
                own_to(k, d).wait_send()
        own_partner(k).wait_send()
        for pp in range(L):
            for ok, to in ((relay_right(pp), p + 1), (relay_left(pp), p - 1)):
                @pl.when(ok)
                def _():
                    relay_copy(k, pp, to).wait_send()

            @pl.when(pp != p)
            def _():
                fwd_copy(k, pp).wait_send()
        return carry

    lax.fori_loop(0, K, drain, 0)


def body(R, Q, trials, valence_orb, conduction_orb, screened):
    NT, vb, cb = trials.shape
    m = valence_orb.shape[1]
    n = conduction_orb.shape[1]
    V, C, L = vb * Q, cb * R, R // 2
    nw = min(256, n)
    K = n // nw
    dma = pltpu.SemaphoreType.DMA
    vm = pl.BlockSpec(memory_space=pltpu.VMEM)
    return pl.pallas_call(
        functools.partial(kernel, R, Q, K),
        out_shape=jax.ShapeDtypeStruct((NT, vb, cb), F32),
        in_specs=[vm, vm, vm, pl.BlockSpec(memory_space=pl.ANY)],
        out_specs=vm,
        scratch_shapes=[
            pltpu.VMEM((R, Q, NT, vb, cb), F32),
            pltpu.VMEM((NT * V, C), BF16),
            pltpu.VMEM((NT * V, C), BF16),
            pltpu.VMEM((Q, vb, m), F32),
            pltpu.VMEM((V, m), BF16),
            pltpu.VMEM((V, m), BF16),
            pltpu.VMEM((m, V), BF16),
            pltpu.VMEM((m, V), BF16),
            pltpu.VMEM((K, R, cb, nw), F32),
            pltpu.VMEM((C, n), BF16),
            pltpu.VMEM((C, n), BF16),
            pltpu.VMEM((2, m, nw), F32),
            pltpu.VMEM((NT * V, n), BF16),
            pltpu.VMEM((NT * V, n), BF16),
            pltpu.VMEM((NT, V, L * cb), F32),
            pltpu.VMEM((NT, V, L * cb), F32),
            pltpu.VMEM((NT, Q, vb, L * cb), F32),
            pltpu.VMEM((NT, Q, vb, L * cb), F32),
            pltpu.VMEM((NT, L, vb, cb), F32),
            pltpu.VMEM((NT, L, vb, cb), F32),
            dma((R, Q)), dma((L,)), dma((L, Q)), dma((L, Q)),
            dma((Q,)), dma((Q,)),
            dma((K, R)), dma((K, 5)), dma((K, L)), dma((K, L)),
            dma((2,)),
            dma((NT,)), dma((NT,)), dma((NT, Q)), dma((NT, Q)), dma((NT, L)), dma((NT, L)),
        ],
        compiler_params=pltpu.CompilerParams(
            collective_id=0, has_side_effects=True, vmem_limit_bytes=67043328
        ),
    )(trials, valence_orb, conduction_orb, screened)


def solution(mesh):
    R, Q = mesh.shape["row"], mesh.shape["col"]
    placed = (P(None, "col", "row"), P("col", "row"), P("row", "col"), P("row", "col"))
    return jax.shard_map(
        functools.partial(body, R, Q), mesh=mesh, in_specs=placed,
        out_specs=P(None, "col", "row"), check_vma=False,
    )
```

profile of v0, /device:TPU:0, one launch (start us, length us, event | category | flops | bytes accessed | tf_op | source)
XLA Modules:
  0.0 167.6 jit_solution(15379586721441646933)
XLA Ops:
  0.0 166.0 %shard_map.46 = f32[2,128,128]{2,1,0:T(8,128)} custom-call(f32[2,128,128]{2,1,0:T(8,128)} %t_ref.1, f32[128,1024]{1,0:T(8,128)} %v_ref.1, f32[128,2048]{1,0:T(8,128)} %co_ref.1, f32[1024,2048]{1,0:T(8,128)} %s_hbm.1), custom_call_target="tpu_custom_call" | custom-call | tf_op jit(solution)/shard_map/pallas_call | solution.py:392
  166.0 1.6 copy.6
where the time goes:
time: 168 us
  Pallas kernels  166 us (99%)
    pallas_call x1, Pallas kernels, body(): pl.pallas_call(functools.partial(kernel, R, Q, K), out_shape=jax.ShapeDty...  166 us

commit v1 on v0

--- a/solution.py
+++ b/solution.py
@@ -27,7 +27,7 @@
     R, Q, K,
     t_ref, v_ref, co_ref, s_hbm, out_ref,
     t_buf, t_hi, t_lo, v_all, v_hi, v_lo, vt_hi, vt_lo, co_buf, co_hi, co_lo, s_buf,
-    u_hi, u_lo, psend, precv, osum, xrecv, zbuf, zrecv,
+    p_hi, p_lo, u_hi, u_lo, psend, precv, osum, xrecv, zbuf, zrecv,
     t_recv, t_zs, t_xs, t_ps, v_recv, v_send, co_recv, co_own, co_rel, co_fwd,
     s_sem, p_send, p_recv, x_send, x_recv, z_send, z_recv,
 ):
@@ -217,11 +217,20 @@
     def project(slot, k, t):
         lanes = lanes_of(k)
         rows = pl.ds(pl.multiple_of(t * V, V), V)
-        pairs = s_buf[slot] * dot3(vt_hi[...], vt_lo[...], u_hi[rows, lanes], u_lo[rows, lanes])
-        p_hi, p_lo = split(pairs)
-        hi, lo = split(dot3(v_hi[...], v_lo[...], p_hi, p_lo))
-        u_hi[rows, lanes] = hi
-        u_lo[rows, lanes] = lo
+        h_hi, h_lo = u_hi[rows, lanes], u_lo[rows, lanes]
+        m = s_buf.shape[1]
+        step = min(256, m)
+        for r in range(0, m, step):
+            block = slice(r, r + step)
+            hi, lo = split(s_buf[slot, block] * dot3(vt_hi[block], vt_lo[block], h_hi, h_lo))
+            p_hi[block] = hi
+            p_lo[block] = lo
+        step = min(256, V)
+        for r in range(0, V, step):
+            hi, lo = split(dot3(v_hi[r : r + step], v_lo[r : r + step], p_hi[...], p_lo[...]))
+            rows = pl.ds(pl.multiple_of(t * V + r, step), step)
+            u_hi[rows, lanes] = hi
+            u_lo[rows, lanes] = lo
 
     more(relay, 2)
     more(forward, 1)
@@ -407,6 +416,8 @@
             pltpu.VMEM((C, n), BF16),
             pltpu.VMEM((C, n), BF16),
             pltpu.VMEM((2, m, nw), F32),
+            pltpu.VMEM((m, nw), BF16),
+            pltpu.VMEM((m, nw), BF16),
             pltpu.VMEM((NT * V, n), BF16),
             pltpu.VMEM((NT * V, n), BF16),
             pltpu.VMEM((NT, V, L * cb), F32),

time: 168 us -> 148 us (0.88)
  Pallas kernels: 166 us -> 146 us
    pallas_call x1, Pallas kernels: 166 us -> 146 us  [body(): pl.pallas_call(functools.partial(kernel, R, Q, K), out_shape=jax.ShapeDty...]
where the time goes in v1:
time: 148 us
  Pallas kernels  146 us (99%)
  local copies, waits for them, and re-layouts  1.57 us (1%)
    pallas_call x1, Pallas kernels, body(): pl.pallas_call(functools.partial(kernel, R, Q, K), out_shape=jax.ShapeDty...  146 us

profile of v1, /device:TPU:0, one launch (start us, length us, event | category | flops | bytes accessed | tf_op | source)
XLA Modules:
  0.0 147.9 jit_solution(5346804678565786489)
XLA Ops:
  0.0 146.4 %shard_map.46 = f32[2,128,128]{2,1,0:T(8,128)} custom-call(f32[2,128,128]{2,1,0:T(8,128)} %t_ref.1, f32[128,1024]{1,0:T(8,128)} %v_ref.1, f32[128,2048]{1,0:T(8,128)} %co_ref.1, f32[1024,2048]{1,0:T(8,128)} %s_hbm.1), custom_call_target="tpu_custom_call" | custom-call | tf_op jit(solution)/shard_map/pallas_call | solution.py:401
  146.4 1.6 %copy.6 = f32[2,128,128]{2,1,0:T(8,128)} copy(f32[2,128,128]{2,1,0:T(8,128)} %shard_map.46) | data formatting | bytes 262144

commit v2 on v1

--- a/solution.py
+++ b/solution.py
@@ -28,7 +28,7 @@
     t_ref, v_ref, co_ref, s_hbm, out_ref,
     t_buf, t_hi, t_lo, v_all, v_hi, v_lo, vt_hi, vt_lo, co_buf, co_hi, co_lo, s_buf,
     p_hi, p_lo, u_hi, u_lo, psend, precv, osum, xrecv, zbuf, zrecv,
-    t_recv, t_zs, t_xs, t_ps, v_recv, v_send, co_recv, co_own, co_rel, co_fwd,
+    t_recv, t_recv2, t_zs, t_xs, t_rs, t_ps, v_recv, v_send, co_recv, co_own, co_rel, co_fwd,
     s_sem, p_send, p_recv, x_send, x_recv, z_send, z_recv,
 ):
     NT, vb, cb = t_ref.shape
@@ -63,14 +63,36 @@
     def t_line(d):
         return remote(t_ref, t_buf.at[mypos, q], t_zs.at[d], t_recv.at[mypos, q], line((p + d) % L))
 
+    square = Q == 4 and vb % 16 == 0
+    sides = (q + 1 - 2 * (q % 2), (q + 2) % 4) if square else ()
+    corner = 3 - q
+    half_rows = [pl.ds(i * (vb // 2), vb // 2) for i in range(2)]
+
+    def t_pos(j):
+        return c * L + (p + L - j) % L
+
     def t_peer(j, d):
-        pos = c * L + (p + L - j) % L
+        pos = t_pos(j)
         src = t_ref if j == 0 else t_buf.at[pos, q]
-        return remote(src, t_buf.at[pos, q], t_xs.at[j, d], t_recv.at[pos, q], peer((q + d) % Q))
+        to = sides[d - 1] if square else (q + d) % Q
+        return remote(src, t_buf.at[pos, q], t_xs.at[j, d], t_recv.at[pos, q], peer(to))
+
+    def t_relay(j, i):
+        part = t_buf.at[t_pos(j), sides[i], :, half_rows[i]]
+        sem = t_recv if i == 0 else t_recv2
+        return remote(part, part, t_rs.at[j, i], sem.at[t_pos(j), sides[i]], peer(sides[1 - i]))
+
+    def t_corner_wait(j):
+        for i in range(2):
+            part = t_buf.at[t_pos(j), corner, :, half_rows[i]]
+            sem = t_recv if i == 0 else t_recv2
+            remote(part, part, t_zs.at[0], sem.at[t_pos(j), corner], partner).wait_recv()
+
+    peers = range(1, 3 if square else Q)
 
     def t_partner(j, d):
         pos = c * L + (p + L - j) % L
-        qq = (q + Q - d) % Q
+        qq = (q, *sides, corner)[d] if square else (q + Q - d) % Q
         src = t_ref if (j == 0 and d == 0) else t_buf.at[pos, qq]
         return remote(src, t_buf.at[pos, qq], t_ps.at[j, d], t_recv.at[pos, qq], partner)
 
@@ -78,7 +100,21 @@
         remote(t_buf.at[pos, qq], t_buf.at[pos, qq], t_zs.at[0], t_recv.at[pos, qq], partner).wait_recv()
 
     def v_peer(d):
-        return remote(v_ref, v_all.at[q], v_send.at[d], v_recv.at[q], peer((q + d) % Q))
+        return remote(v_ref, v_all.at[q], v_send.at[d, 0], v_recv.at[q, 0], peer((q + d) % Q))
+
+    def v_side(i, part):
+        rows = half_rows[part]
+        return remote(
+            v_ref.at[rows], v_all.at[q, rows], v_send.at[i, part], v_recv.at[q, part], peer(sides[i])
+        )
+
+    def v_relay(i):
+        part = v_all.at[sides[i], half_rows[i]]
+        return remote(part, part, v_send.at[2, i], v_recv.at[sides[i], i], peer(sides[1 - i]))
+
+    def v_wait(qq, part):
+        rows = v_all.at[qq, half_rows[part]]
+        remote(rows, rows, v_send.at[0, 0], v_recv.at[qq, part], partner).wait_recv()
 
     def own_to(k, d):
         lanes = pl.ds(pl.multiple_of(k * nw, nw), nw)
@@ -151,9 +187,12 @@
 
     for d in range(1, L):
         t_line(d).start()
-    for d in range(1, Q):
+    for d in peers:
         t_peer(0, d).start()
     t_partner(0, 0).start()
+    if square:
+        for i in range(2):
+            v_side(i, i).start()
     ahead = [0]
 
     def more_own(k):
@@ -172,18 +211,35 @@
     for k in range(K):
         co_buf[k, mypos] = co_ref[:, k * nw : (k + 1) * nw]
     for j in range(1, L):
-        t_wait(c * L + (p + L - j) % L, q)
-        for d in range(1, Q):
+        t_wait(t_pos(j), q)
+        for d in peers:
             t_peer(j, d).start()
         t_partner(j, 0).start()
-    for d in range(1, Q):
-        v_peer(d).start()
-    more(relay, 0)
-    more_own(4)
-    for j in range(L):
+    if square:
+        for i in range(2):
+            v_side(i, 1 - i).start()
+        more(relay, 0)
+        more_own(4)
+        for j in range(L):
+            for i in range(2):
+                t_wait(t_pos(j), sides[i])
+                t_relay(j, i).start()
+                t_partner(j, 1 + i).start()
+        for i in range(2):
+            v_wait(sides[i], i)
+            v_relay(i).start()
+        for j in range(L):
+            t_corner_wait(j)
+            t_partner(j, 3).start()
+    else:
         for d in range(1, Q):
-            t_wait(c * L + (p + L - j) % L, (q + Q - d) % Q)
-            t_partner(j, d).start()
+            v_peer(d).start()
+        more(relay, 0)
+        more_own(4)
+        for j in range(L):
+            for d in range(1, Q):
+                t_wait(t_pos(j), (q + Q - d) % Q)
+                t_partner(j, d).start()
     more(relay, 1)
     more(forward, 0)
     more_own(5)
@@ -232,17 +288,20 @@
             u_hi[rows, lanes] = hi
             u_lo[rows, lanes] = lo
 
+    more_own(6)
+    encode_half(0)
     more(relay, 2)
     more(forward, 1)
-    more_own(6)
-    encode_half(0)
-    more(relay, 3)
-    more(forward, 2)
     more_own(7)
-    more(encode_half, 1)
-    for d in range(1, Q):
-        qq = (q + Q - d) % Q
-        remote(v_all.at[qq], v_all.at[qq], v_send.at[0], v_recv.at[qq], partner).wait_recv()
+    if square:
+        for i in range(2):
+            v_wait(sides[i], 1 - i)
+        for i in range(2):
+            v_wait(corner, i)
+    else:
+        for d in range(1, Q):
+            qq = (q + Q - d) % Q
+            remote(v_all.at[qq], v_all.at[qq], v_send.at[0, 0], v_recv.at[qq, 0], partner).wait_recv()
     for qq in range(Q):
         hi, lo = split(v_all[qq])
         v_hi[qq * vb : (qq + 1) * vb, :] = hi
@@ -265,17 +324,17 @@
         def _():
             send_own(s + 7)
 
-        @pl.when(s + 4 < K)
-        def _():
-            relay(s + 4)
-
         @pl.when(s + 3 < K)
         def _():
-            forward(s + 3)
+            relay(s + 3)
 
         @pl.when(s + 2 < K)
         def _():
-            encode_half(s + 2)
+            forward(s + 2)
+
+        @pl.when(s + 1 < K)
+        def _():
+            encode_half(s + 1)
 
         s_copy(s, s % 2).wait()
         next_screened(s)
@@ -358,14 +417,24 @@
         for t in range(NT):
             z_copy(t, d).wait_send()
     for d in range(1, Q):
-        v_peer(d).wait_send()
         for t in range(NT):
             x_copy(t, d).wait_send()
+    if square:
+        for i in range(2):
+            v_relay(i).wait_send()
+            for part in range(2):
+                v_side(i, part).wait_send()
+    else:
+        for d in range(1, Q):
+            v_peer(d).wait_send()
     for t in range(NT):
         p_copy(t).wait_send()
     for j in range(L):
-        for d in range(1, Q):
+        for d in peers:
             t_peer(j, d).wait_send()
+        if square:
+            for i in range(2):
+                t_relay(j, i).wait_send()
         for d in range(Q):
             t_partner(j, d).wait_send()
 
@@ -426,8 +495,8 @@
             pltpu.VMEM((NT, Q, vb, L * cb), F32),
             pltpu.VMEM((NT, L, vb, cb), F32),
             pltpu.VMEM((NT, L, vb, cb), F32),
-            dma((R, Q)), dma((L,)), dma((L, Q)), dma((L, Q)),
-            dma((Q,)), dma((Q,)),
+            dma((R, Q)), dma((R, Q)), dma((L,)), dma((L, Q)), dma((L, 2)), dma((L, Q)),
+            dma((Q, 2)), dma((Q, 2)),
             dma((K, R)), dma((K, 5)), dma((K, L)), dma((K, L)),
             dma((2,)),
             dma((NT,)), dma((NT,)), dma((NT, Q)), dma((NT, Q)), dma((NT, L)), dma((NT, L)),

time: 148 us -> 144 us (0.973)
  Pallas kernels: 146 us -> 142 us
    pallas_call x1, Pallas kernels: 146 us -> 142 us  [body(): pl.pallas_call(functools.partial(kernel, R, Q, K), out_shape=jax.ShapeDty...]
where the time goes in v2:
time: 144 us
  Pallas kernels  142 us (99%)
  local copies, waits for them, and re-layouts  1.57 us (1%)
    pallas_call x1, Pallas kernels, body(): pl.pallas_call(functools.partial(kernel, R, Q, K), out_shape=jax.ShapeDty...  142 us

profile of v2, /device:TPU:0, one launch (start us, length us, event | category | flops | bytes accessed | tf_op | source)
XLA Modules:
  0.0 143.6 jit_solution(12486556324594428680)
XLA Ops:
  0.0 142.0 %shard_map.46 = f32[2,128,128]{2,1,0:T(8,128)} custom-call(f32[2,128,128]{2,1,0:T(8,128)} %t_ref.1, f32[128,1024]{1,0:T(8,128)} %v_ref.1, f32[128,2048]{1,0:T(8,128)} %co_ref.1, f32[1024,2048]{1,0:T(8,128)} %s_hbm.1), custom_call_target="tpu_custom_call" | custom-call | tf_op jit(solution)/shard_map/pallas_call | solution.py:470
  142.0 1.6 %copy.6 = f32[2,128,128]{2,1,0:T(8,128)} copy(f32[2,128,128]{2,1,0:T(8,128)} %shard_map.46) | data formatting | bytes 262144

commit v3 on v2

--- a/solution.py
+++ b/solution.py
@@ -349,39 +349,63 @@
 
     half_c = L * cb
 
-    def decode(t, par):
-        rows = slice(t * V, (t + 1) * V)
+    parts = 2 if Q % 2 == 0 else 1
+    pq = Q // parts
+    pv = V // parts
+
+    def side_of(h):
+        return (q // pq + parts - 1 - h) % parts
+
+    def part_rows(h):
+        return pl.ds(pl.multiple_of(side_of(h) * pv, pv), pv)
+
+    def decode(t, par, h):
+        rows = pl.ds(pl.multiple_of(t * V + side_of(h) * pv, pv), pv)
         cols = pl.ds(pl.multiple_of(par * half_c, half_c), half_c)
         return dot3(u_hi[rows, :], u_lo[rows, :], co_hi[cols, :], co_lo[cols, :], ((1,), (1,)))
 
-    def p_copy(t):
-        return remote(psend.at[t], precv.at[t], p_send.at[t], p_recv.at[t], partner)
-
-    def x_copy(t, d):
-        to = (q + d) % Q
-        return remote(osum.at[t, to], xrecv.at[t, d], x_send.at[t, d], x_recv.at[t, d], peer(to))
+    def p_copy(t, h):
+        rows = part_rows(h)
+        return remote(psend.at[t, rows], precv.at[t, rows], p_send.at[t, h], p_recv.at[t, h], partner)
+
+    def peer_at(h, i):
+        return side_of(h) * pq + (q + i) % pq
+
+    def x_copy(t, h, i):
+        to = peer_at(h, i)
+        e = h * pq + i
+        return remote(osum.at[t, to], xrecv.at[t, e], x_send.at[t, e], x_recv.at[t, e], peer(to))
+
+    hops = [(h, i) for h in range(parts) for i in range(pq) if h < parts - 1 or i > 0]
+
+    def x_wait(t, h, i):
+        e = h * pq + i
+        remote(xrecv.at[t, e], xrecv.at[t, e], x_send.at[t, e], x_recv.at[t, e], partner).wait_recv()
 
     def z_copy(t, d):
         to = (p + d) % L
         return remote(zbuf.at[t, to], zrecv.at[t, d], z_send.at[t, d], z_recv.at[t, d], line(to))
 
-    def to_partner(t):
-        psend[t] = decode(t, 1 - c)
-        p_copy(t).start()
-
-    def to_peers(t):
-        own = decode(t, c)
-        p_copy(t).wait_recv()
-        for qq in range(Q):
-            osum[t, qq] = own[qq * vb : (qq + 1) * vb, :] + precv[t, qq * vb : (qq + 1) * vb, :]
-        for d in range(Q - 1, 0, -1):
-            x_copy(t, d).start()
+    def to_partner(t, h):
+        psend[t, part_rows(h)] = decode(t, 1 - c, h)
+        p_copy(t, h).start()
+
+    def to_peers(t, h):
+        own = decode(t, c, h)
+        p_copy(t, h).wait_recv()
+        for i in range(pq):
+            qq = side_of(h) * pq + i
+            rows = pl.ds(pl.multiple_of(qq * vb, vb), vb)
+            osum[t, qq] = own[i * vb : (i + 1) * vb, :] + precv[t, rows, :]
+        for g, i in hops:
+            if g == h:
+                x_copy(t, g, i).start()
 
     def to_line(t):
         total = osum[t, q]
-        for d in range(Q - 1, 0, -1):
-            x_copy(t, d).wait_recv()
-            total = total + xrecv[t, d]
+        for h, i in hops:
+            x_wait(t, h, i)
+            total = total + xrecv[t, h * pq + i]
         for pp in range(L):
             zbuf[t, pp] = total[:, pp * cb : (pp + 1) * cb]
         for d in range(1, L):
@@ -404,10 +428,13 @@
                 return carry
 
             lax.fori_loop(0, K - both, later_stage, 0)
-        to_partner(t)
+        to_partner(t, 0)
         if t > 0:
             to_line(t - 1)
-        to_peers(t)
+        for h in range(parts):
+            to_peers(t, h)
+            if h + 1 < parts:
+                to_partner(t, h + 1)
     to_line(NT - 1)
     for t in range(NT):
         finish(t)
@@ -416,9 +443,9 @@
         t_line(d).wait_send()
         for t in range(NT):
             z_copy(t, d).wait_send()
-    for d in range(1, Q):
-        for t in range(NT):
-            x_copy(t, d).wait_send()
+    for t in range(NT):
+        for h, i in hops:
+            x_copy(t, h, i).wait_send()
     if square:
         for i in range(2):
             v_relay(i).wait_send()
@@ -428,7 +455,8 @@
         for d in range(1, Q):
             v_peer(d).wait_send()
     for t in range(NT):
-        p_copy(t).wait_send()
+        for h in range(parts):
+            p_copy(t, h).wait_send()
     for j in range(L):
         for d in peers:
             t_peer(j, d).wait_send()
@@ -499,7 +527,7 @@
             dma((Q, 2)), dma((Q, 2)),
             dma((K, R)), dma((K, 5)), dma((K, L)), dma((K, L)),
             dma((2,)),
-            dma((NT,)), dma((NT,)), dma((NT, Q)), dma((NT, Q)), dma((NT, L)), dma((NT, L)),
+            dma((NT, 2)), dma((NT, 2)), dma((NT, Q)), dma((NT, Q)), dma((NT, L)), dma((NT, L)),
         ],
         compiler_params=pltpu.CompilerParams(
             collective_id=0, has_side_effects=True, vmem_limit_bytes=67043328

time: 144 us -> 140 us (0.972)
  Pallas kernels: 142 us -> 138 us
    pallas_call x1, Pallas kernels: 142 us -> 138 us  [body(): pl.pallas_call(functools.partial(kernel, R, Q, K), out_shape=jax.ShapeDty...]
where the time goes in v3:
time: 140 us
  Pallas kernels  138 us (99%)
  local copies, waits for them, and re-layouts  1.57 us (1%)
    pallas_call x1, Pallas kernels, body(): pl.pallas_call(functools.partial(kernel, R, Q, K), out_shape=jax.ShapeDty...  138 us

profile of v3, /device:TPU:0, one launch (start us, length us, event | category | flops | bytes accessed | tf_op | source)
XLA Modules:
  0.0 139.7 jit_solution(7864112395592322872)
XLA Ops:
  0.0 138.2 %shard_map.46 = f32[2,128,128]{2,1,0:T(8,128)} custom-call(f32[2,128,128]{2,1,0:T(8,128)} %t_ref.1, f32[128,1024]{1,0:T(8,128)} %v_ref.1, f32[128,2048]{1,0:T(8,128)} %co_ref.1, f32[1024,2048]{1,0:T(8,128)} %s_hbm.1), custom_call_target="tpu_custom_call" | custom-call | tf_op jit(solution)/shard_map/pallas_call | solution.py:498
  138.2 1.6 %copy.6 = f32[2,128,128]{2,1,0:T(8,128)} copy(f32[2,128,128]{2,1,0:T(8,128)} %shard_map.46) | data formatting | bytes 262144

commit v4 on v3

--- a/solution.py
+++ b/solution.py
@@ -293,6 +293,7 @@
     more(relay, 2)
     more(forward, 1)
     more_own(7)
+    more(encode_half, 1)
     if square:
         for i in range(2):
             v_wait(sides[i], 1 - i)
@@ -332,10 +333,6 @@
         def _():
             forward(s + 2)
 
-        @pl.when(s + 1 < K)
-        def _():
-            encode_half(s + 1)
-
         s_copy(s, s % 2).wait()
         next_screened(s)
 
@@ -343,7 +340,13 @@
             project(s % 2, s, t)
             return carry
 
-        return lax.fori_loop(0, jnp.where(s < both, NT, 1), one, carry)
+        carry = lax.fori_loop(0, jnp.where(s < both, NT, 1), one, carry)
+
+        @pl.when(s + 2 < K)
+        def _():
+            encode_half(s + 2)
+
+        return carry
 
     lax.fori_loop(0, K, stage, 0)
 

time: 140 us -> 138 us (0.986)
  Pallas kernels: 138 us -> 136 us
    pallas_call x1, Pallas kernels: 138 us -> 136 us  [body(): pl.pallas_call(functools.partial(kernel, R, Q, K), out_shape=jax.ShapeDty...]
where the time goes in v4:
time: 138 us
  Pallas kernels  136 us (99%)
  local copies, waits for them, and re-layouts  1.57 us (1%)
    pallas_call x1, Pallas kernels, body(): pl.pallas_call(functools.partial(kernel, R, Q, K), out_shape=jax.ShapeDty...  136 us

profile of v4, /device:TPU:0, one launch (start us, length us, event | category | flops | bytes accessed | tf_op | source)
XLA Modules:
  0.0 137.9 jit_solution(2359254308226531934)
XLA Ops:
  0.0 136.3 %shard_map.46 = f32[2,128,128]{2,1,0:T(8,128)} custom-call(f32[2,128,128]{2,1,0:T(8,128)} %t_ref.1, f32[128,1024]{1,0:T(8,128)} %v_ref.1, f32[128,2048]{1,0:T(8,128)} %co_ref.1, f32[1024,2048]{1,0:T(8,128)} %s_hbm.1), custom_call_target="tpu_custom_call" | custom-call | tf_op jit(solution)/shard_map/pallas_call | solution.py:501
  136.4 1.6 %copy.6 = f32[2,128,128]{2,1,0:T(8,128)} copy(f32[2,128,128]{2,1,0:T(8,128)} %shard_map.46) | data formatting | bytes 262144
